TPU v7x, 256 devices: a whole 4x4x8 slice. The times are simulated.
256 devices in a mesh: px: 16 (over z, y_hi), py: 16 (over x, y_lo, core).
Axes of the slice: x: 4, y: 4 (y_hi: 2, y_lo: 2; y = y_hi * 2 + y_lo), z: 8, core: 2. Of those that a mesh axis runs over, the one named last changes fastest.
Arguments:
- estimate: float32 [512, 512, 128], P('px', 'py'), may hold values from 0.2 to 5
- observed: float32 [512, 512, 128], P('px', 'py'), may hold values from 0.2 to 5
- psf: float32 [32, 32, 32], replicated, as said below
Outputs:
- updated: float32 [512, 512, 128], P('px', 'py')
Inputs may be any that keep to these rules, and one draw needn't show every extreme that they name: `psf`: every entry is positive.
All inputs are finite; a program needn't handle non-finite values.
Results may differ from a plain program's by a relative error of at most 0.00009.
Values sent between devices are 32-bit elements; how exact they have to be, the bound alone decides.
No kernel may reach another device: no remote copies, remote signals or barrier semaphores. Data moves between devices by JAX's collectives and lax.ppermute only.
A program may use at most 128 MiB of HBM per device.

v0:
```python
import math
import jax
import jax.numpy as jnp
from jax import lax
from jax.sharding import PartitionSpec as P

NX = 512
NY = 512
penalty_weight = 0.1
smoothing = 0.1


def with_halo(block, sides, width):
    for axis, dim in sides:
        count = lax.axis_size(axis)
        forward = [(i, i + 1) for i in range(count - 1)]
        backward = [(target, source) for source, target in forward]
        low = lax.ppermute(
            lax.slice_in_dim(block, block.shape[dim] - width, None, axis=dim), axis, forward
        )
        high = lax.ppermute(lax.slice_in_dim(block, 0, width, axis=dim), axis, backward)
        block = jnp.concatenate([low, block, high], axis=dim)
    return block


def product(pattern, left, right):
    return jnp.einsum(pattern, left, right, precision=lax.Precision.HIGHEST)


def tables(length):
    indices = jnp.arange(length)
    turns = jnp.remainder(indices[:, None] * indices[None, :], length).astype(jnp.float32) * (
        2.0 * math.pi / length
    )
    return (jnp.cos(turns), jnp.sin(turns))


def offset_tables(offsets, frequency, length):
    turns = jnp.remainder(offsets[:, None] * frequency[None, :], length).astype(jnp.float32) * (
        2.0 * math.pi / length
    )
    return (jnp.cos(turns), jnp.sin(turns))


def complex_apply(real_part, imag_part, cosine, sines, pattern, forward):
    real_cos = product(pattern, real_part, cosine)
    real_sin = product(pattern, real_part, sines)
    imag_cos = product(pattern, imag_part, cosine)
    imag_sin = product(pattern, imag_part, sines)
    if forward:
        return (real_cos + imag_sin, imag_cos - real_sin)
    return (real_cos - imag_sin, imag_cos + real_sin)


def transfer_function(
    kernel, first_index, second_index, depth_share, first_share, second_whole, first_whole, depth
):
    length = kernel.shape[0]
    offsets = jnp.arange(length) - length // 2
    depth_freq = first_index * depth_share + jnp.arange(depth_share)
    first_freq = second_index * first_share + jnp.arange(first_share)
    second_freq = jnp.arange(second_whole)
    cosine, sines = offset_tables(offsets, depth_freq, depth)
    real_part = product("baz,zk->bak", kernel, cosine)
    imag_part = -product("baz,zk->bak", kernel, sines)
    cosine, sines = offset_tables(offsets, first_freq, first_whole)
    real_part, imag_part = complex_apply(real_part, imag_part, cosine, sines, "baz,aj->bzj", True)
    cosine, sines = offset_tables(offsets, second_freq, second_whole)
    real_part, imag_part = complex_apply(real_part, imag_part, cosine, sines, "bzj,bm->zjm", True)
    factor = 1.0 / (first_whole * second_whole * depth)
    return (real_part * factor, imag_part * factor)


def outward_one(spectrum, handler):
    result = handler(lax.all_to_all(spectrum, "py", split_axis=2, concat_axis=3, tiled=True))
    return result


def outward_two(spectrum):
    result = lax.all_to_all(spectrum, "px", split_axis=2, concat_axis=3, tiled=True)
    return result


def homeward_two(spectrum, handler):
    result = handler(lax.all_to_all(spectrum, "px", split_axis=3, concat_axis=2, tiled=True))
    return result


def homeward_one(spectrum, handler):
    result = handler(lax.all_to_all(spectrum, "py", split_axis=3, concat_axis=2, tiled=True))
    return result


def along_first(segment):
    cosine, sines = tables(segment.shape[3])
    real_part, imag_part = complex_apply(segment[0], segment[1], cosine, sines, "bza,ak->zkb", True)
    return jnp.stack([real_part, imag_part])


def inverse_first(segment):
    cosine, sines = tables(segment.shape[2])
    real_part, imag_part = complex_apply(
        segment[0], segment[1], cosine, sines, "zab,ak->bzk", False
    )
    return jnp.stack([real_part, imag_part])


def to_real(segment):
    cosine, sines = tables(segment.shape[2])
    return product("bza,zk->bak", segment[0], cosine) - product("bza,zk->bak", segment[1], sines)


def convolve(volume, transfer_real, transfer_imag, adjoint):
    cosine, sines = tables(volume.shape[2])
    spectrum = jnp.stack(
        [product("baz,zk->bka", volume, cosine), -product("baz,zk->bka", volume, sines)]
    )
    spectrum = outward_one(spectrum, along_first)
    spectrum = outward_two(spectrum)
    cosine_second, sines_second = tables(spectrum.shape[3])
    real_part, imag_part = complex_apply(
        spectrum[0], spectrum[1], cosine_second, sines_second, "zab,bk->zak", True
    )
    signed_imag = -transfer_imag if adjoint else transfer_imag
    weighted_real = real_part * transfer_real - imag_part * signed_imag
    weighted_imag = real_part * signed_imag + imag_part * transfer_real
    real_part, imag_part = complex_apply(
        weighted_real, weighted_imag, cosine_second, sines_second, "zab,bk->zak", False
    )
    spectrum = homeward_two(jnp.stack([real_part, imag_part]), inverse_first)
    return homeward_one(spectrum, to_real)


def backward_depth(flux):
    return flux - jnp.concatenate([jnp.zeros_like(flux[:, :, :1]), flux[:, :, :-1]], 2)


def normalized(slope_rows, slope_cols, slope_depth):
    factor = lax.rsqrt(
        slope_rows * slope_rows
        + slope_cols * slope_cols
        + slope_depth * slope_depth
        + smoothing * smoothing
    )
    return (slope_rows * factor, slope_cols * factor, slope_depth * factor)


def variation(volume):
    row_count = volume.shape[0]
    col_count = volume.shape[1]
    padded = with_halo(volume, (("px", 0), ("py", 1)), 1)
    region = padded[:-1, :-1]
    slope_rows = padded[1:, :-1] - region
    slope_cols = padded[:-1, 1:] - region
    row_global = lax.axis_index("px") * row_count - 1 + jnp.arange(row_count + 1)
    col_global = lax.axis_index("py") * col_count - 1 + jnp.arange(col_count + 1)
    row_valid = ((row_global >= 0) & (row_global <= NX - 2))[:, None, None]
    col_valid = ((col_global >= 0) & (col_global <= NY - 2))[None, :, None]
    slope_rows = jnp.where(row_valid, slope_rows, 0.0)
    slope_cols = jnp.where(col_valid, slope_cols, 0.0)
    slope_depth = jnp.concatenate(
        [region[:, :, 1:] - region[:, :, :-1], jnp.zeros_like(region[:, :, :1])], 2
    )
    flux_rows, flux_cols, flux_depth = normalized(slope_rows, slope_cols, slope_depth)
    divergence = (
        flux_rows[1:, 1:]
        - flux_rows[:-1, 1:]
        + (flux_cols[1:, 1:] - flux_cols[1:, :-1])
        + backward_depth(flux_depth[1:, 1:])
    )
    return divergence


def shards(estimate, observed, psf):
    first_index = lax.axis_index("py")
    second_index = lax.axis_index("px")
    first_size = lax.axis_size("py")
    second_size = lax.axis_size("px")
    second_local, first_local, depth = estimate.shape
    first_whole = first_local * first_size
    second_whole = second_local * second_size
    transfer_real, transfer_imag = transfer_function(
        psf,
        first_index,
        second_index,
        depth // first_size,
        first_whole // second_size,
        second_whole,
        first_whole,
        depth,
    )
    blurred = convolve(estimate, transfer_real, transfer_imag, False)
    quotient = observed / blurred
    correction = convolve(quotient, transfer_real, transfer_imag, True)
    divergence = variation(estimate)
    return estimate * correction / (1.0 - penalty_weight * divergence)


def solution(mesh):
    placed = (P("px", "py", None), P("px", "py", None), P())
    return jax.shard_map(
        shards, mesh=mesh, in_specs=placed, out_specs=P("px", "py", None), check_vma=False
    )
```

profile of v0, /device:TPU:2, one launch (start us, length us, event | category | flops | bytes accessed | tf_op | source)
XLA Modules:
  0.0 613.5 jit_solution(9039552779921789667)
XLA Ops:
  13.1 6.1 all-to-all-start
  21.4 12.0 %all-to-all-done = f32[16,1,16384]{2,1,0:T(1,128)S(1)} async-done(((f32[16,1,16384]{2,1,0:T(1,128)}), f32[16,1,16384]{2,1,0:T(1,128)S(1)}, u32[]{:S(2)}, u32[]{:S(2)}) %all-to-all-start) | async-done | bytes 1048608 | tf_op jit(solution)/shard_map/all_to_all | solution.py:75
  47.5 6.0 fusion.59
  55.6 6.5 %fusion.57 = f32[512,32,8]{0,1,2:T(8,128)S(1)} fusion(f32[32,8,512]{2,0,1:T(8,128)} %squeeze.49), kind=kOutput, calls=%fused_computation.103 | convolution fusion | flops 808976384 | bytes 1048576 | tf_op jit(solution)/shard_map/bza,ak->zkb/dot_general | solution.py:27
  81.4 11.3 %all-to-all-start.1 = ((f32[16,1,16384]{2,1,0:T(1,128)}), f32[16,1,16384]{2,1,0:T(1,128)S(1)}, u32[]{:S(2)}, u32[]{:S(2)}) async-start(f32[16,1,16384]{2,1,0:T(1,128)} %reshape.86), calls=%async_computation.1 | async-start | bytes 2097152 | tf_op jit(solution)/shard_map/all_to_all | solution.py:80
  101.6 20.9 %all-to-all-done.1 = f32[16,1,16384]{2,1,0:T(1,128)S(1)} async-done(((f32[16,1,16384]{2,1,0:T(1,128)}), f32[16,1,16384]{2,1,0:T(1,128)S(1)}, u32[]{:S(2)}, u32[]{:S(2)}) %all-to-all-start.1) | async-done | bytes 1048608 | tf_op jit(solution)/shard_map/all_to_all | solution.py:80
  137.2 5.8 fusion.55
  154.6 5.7 multiply_subtract_fusion.1
  176.3 5.8 fusion.8
  189.7 33.3 %all_to_all.120 = f32[16,1,16384]{2,1,0:T(1,128)S(1)} all-to-all(f32[16,1,16384]{2,1,0:T(1,128)S(1)} %reshape.88), channel_id=1, replica_groups=mesh['px'=16,'py'=16] {'px'}, dimensions={0} | all-to-all | bytes 2097152 | tf_op jit(solution)/shard_map/all_to_all | solution.py:85
  237.6 5.9 fusion.109
  268.4 19.6 %all_to_all.121 = f32[16,1,16384]{2,1,0:T(1,128)S(1)} all-to-all(f32[16,1,16384]{2,1,0:T(1,128)S(1)} %reshape.90), channel_id=1, replica_groups=mesh['px'=16,'py'=16] {'py'}, dimensions={0} | all-to-all | bytes 2097152 | tf_op jit(solution)/shard_map/all_to_all | solution.py:90
  294.0 6.2 %copy.73 = f32[2,32,8,16,32]{4,2,3,1,0:T(8,128)} copy(f32[2,32,8,16,32]{1,2,0,4,3:T(8,128)} %bitcast.349) | data formatting | bytes 2097152 | tf_op jit(solution)/shard_map/all_to_all | solution.py:90
  320.4 19.2 %all_to_all.122 = f32[16,1,16384]{2,1,0:T(1,128)S(1)} all-to-all(f32[16,1,16384]{2,1,0:T(1,128)S(1)} %reshape.92), channel_id=1, replica_groups=mesh['px'=16,'py'=16] {'py'}, dimensions={0} | all-to-all | bytes 2097152 | tf_op jit(solution)/shard_map/all_to_all | solution.py:75
  353.1 5.9 fusion.47
  384.2 34.2 %all_to_all.123 = f32[16,1,16384]{2,1,0:T(1,128)S(1)} all-to-all(f32[16,1,16384]{2,1,0:T(1,128)S(1)} %reshape.94), channel_id=1, replica_groups=mesh['px'=16,'py'=16] {'px'}, dimensions={0} | all-to-all | bytes 2097152 | tf_op jit(solution)/shard_map/all_to_all | solution.py:80
  433.0 5.8 fusion.43
  496.4 5.7 collective-permute-done.1
  502.9 16.5 %all-to-all-done.6 = f32[16,1,16384]{2,1,0:T(1,128)S(1)} async-done(((f32[16,1,16384]{2,1,0:T(1,128)}), f32[16,1,16384]{2,1,0:T(1,128)S(1)}, u32[]{:S(2)}, u32[]{:S(2)}) %all-to-all-start.6) | async-done | bytes 1048608 | tf_op jit(solution)/shard_map/all_to_all | solution.py:85
  534.4 5.9 fusion.113
  540.2 5.8 fusion.95
  577.7 7.7 %collective-permute-done.2 = f32[34,1,128]{2,1,0:T(1,128)S(1)} collective-permute-done((f32[34,1,128]{2,1,0:T(1,128)S(1)}, f32[34,1,128]{2,1,0:T(1,128)S(1)}, u32[]{:S(2)}, u32[]{:S(2)}) %collective-permute-start.2) | collective-permute-done | bytes 17440 | tf_op jit(solution)/shard_map/ppermute | solution.py:18
  595.9 6.1 copy.85
  607.1 6.2 %fusion.19 = f32[32,32,128]{2,1,0:T(8,128)} fusion(f32[32,32,128]{2,1,0:T(8,128)S(1)} %copy-done.2, f32[32,32,128]{2,1,0:T(8,128)S(1)} %fusion, f32[2,32,16,8,32]{4,3,2,1,0:T(8,128)} %bitcast.355, f32[33,33,128]{2,1,0:T(8,128)S(1)} %get-tuple-element.25, f32[33,33,128]{2,1,0:T(8,128)S(1)} %get-tuple-element.24, f32[33,33,128]{2,1,0:T(8,128)S(1)} %copy-done.7, ...), kind=kOutput, calls=%fused_computation.53 | convolution fusion | flops 202866688 | bytes 6815744 | tf_op jit(solution)/shard_map/bza,zk->bak/dot_general | solution.py:27
  (175 shorter events, 348.4 us)
Async XLA Ops:
  0.0 19.2 %copy-start = (f32[32,32,32]{2,1,0:T(8,128)S(1)}, f32[32,32,32]{2,1,0:T(8,128)}, u32[]{:S(2)}) copy-start(f32[32,32,32]{2,1,0:T(8,128)} %param.5) | copy-start | bytes 393220
  13.1 20.4 %all-to-all-start = ((f32[16,1,16384]{2,1,0:T(1,128)}), f32[16,1,16384]{2,1,0:T(1,128)S(1)}, u32[]{:S(2)}, u32[]{:S(2)}) async-start(f32[16,1,16384]{2,1,0:T(1,128)} %reshape.84), calls=%async_computation | async-start | bytes 2097152 | tf_op jit(solution)/shard_map/all_to_all | solution.py:75
  47.5 6.1 copy-start.3
  55.6 6.5 %copy-start.12 = (f32[32,8,512]{2,0,1:T(8,128)S(1)}, f32[32,8,512]{2,0,1:T(8,128)}, u32[]{:S(2)}) copy-start(f32[32,8,512]{2,0,1:T(8,128)} %squeeze.49) | copy-start | bytes 1572868
  55.6 6.5 %copy-start.17 = (f32[512,32,8]{0,1,2:T(8,128)S(1)}, f32[512,32,8]{0,1,2:T(8,128)}, u32[]{:S(2)}) copy-start(f32[512,32,8]{0,1,2:T(8,128)} %fusion.59) | copy-start | bytes 1572868
  81.4 41.2 %all-to-all-start.1 = ((f32[16,1,16384]{2,1,0:T(1,128)}), f32[16,1,16384]{2,1,0:T(1,128)S(1)}, u32[]{:S(2)}, u32[]{:S(2)}) async-start(f32[16,1,16384]{2,1,0:T(1,128)} %reshape.86), calls=%async_computation.1 | async-start | bytes 2097152 | tf_op jit(solution)/shard_map/all_to_all | solution.py:80
  143.8 10.7 %copy-start.13 = (f32[8,32,512]{2,1,0:T(8,128)S(1)}, f32[8,32,512]{2,1,0:T(8,128)}, u32[]{:S(2)}) copy-start(f32[8,32,512]{2,1,0:T(8,128)} %fusion.16) | copy-start | bytes 1572868
  143.9 10.7 %copy-start.15 = (f32[8,32,512]{2,1,0:T(8,128)S(1)}, f32[8,32,512]{2,1,0:T(8,128)}, u32[]{:S(2)}) copy-start(f32[8,32,512]{2,1,0:T(8,128)} %fusion.17) | copy-start | bytes 1572868
  249.8 10.8 %copy-start.10 = (f32[512,256]{0,1:S(1)}, f32[512,256]{0,1}, u32[]{:S(2)}) copy-start(f32[512,256]{0,1} %fusion.109) | copy-start | bytes 1572868
  294.0 11.2 %copy-start.8 = (f32[32,32,128]{2,1,0:T(8,128)S(1)}, f32[32,32,128]{2,1,0:T(8,128)}, u32[]{:S(2)}) copy-start(f32[32,32,128]{2,1,0:T(8,128)} %param.4) | copy-start | bytes 1572868
  353.1 5.9 copy-start.4
  439.6 10.9 %copy-start.14 = (f32[8,32,512]{2,1,0:T(8,128)S(1)}, f32[8,32,512]{2,1,0:T(8,128)}, u32[]{:S(2)}) copy-start(f32[8,32,512]{2,1,0:T(8,128)} %fusion.16) | copy-start | bytes 1572868
  439.6 10.9 %copy-start.16 = (f32[8,32,512]{2,1,0:T(8,128)S(1)}, f32[8,32,512]{2,1,0:T(8,128)}, u32[]{:S(2)}) copy-start(f32[8,32,512]{2,1,0:T(8,128)} %fusion.17) | copy-start | bytes 1572868
  481.3 8.4 %copy-start.2 = (f32[32,32,128]{2,1,0:T(8,128)S(1)}, f32[32,32,128]{2,1,0:T(8,128)}, u32[]{:S(2)}) copy-start(f32[32,32,128]{2,1,0:T(8,128)} %param.3) | copy-start | bytes 1572868
  486.1 33.3 %all-to-all-start.6 = ((f32[16,1,16384]{2,1,0:T(1,128)}), f32[16,1,16384]{2,1,0:T(1,128)S(1)}, u32[]{:S(2)}, u32[]{:S(2)}) async-start(f32[16,1,16384]{2,1,0:T(1,128)} %reshape.96), calls=%async_computation.6 | async-start | bytes 2097152 | tf_op jit(solution)/shard_map/all_to_all | solution.py:85
  489.8 6.6 %collective-permute-start = (f32[1,32,128]{2,1,0:T(8,128)S(1)}, f32[1,32,128]{2,1,0:T(8,128)S(1)}, u32[]{:S(2)}, u32[]{:S(2)}) collective-permute-start(f32[1,32,128]{2,1,0:T(8,128)S(1)} %get-tuple-element.29), channel_id=1, source_target_pairs={{0,16},{16,32},{32,48},{48,64},{64,80},{80,96},{96,112},{112,128},... | collective-permute-start | bytes 49160 | tf_op jit(solution)/shard_map/ppermute | solution.py:18
  495.0 7.1 %collective-permute-start.1 = (f32[1,32,128]{2,1,0:T(8,128)S(1)}, f32[1,32,128]{2,1,0:T(8,128)S(1)}, u32[]{:S(2)}, u32[]{:S(2)}) collective-permute-start(f32[1,32,128]{2,1,0:T(8,128)S(1)} %get-tuple-element.28), channel_id=1, source_target_pairs={{16,0},{32,16},{48,32},{64,48},{80,64},{96,80},{112,96},{128,112},... | collective-permute-start | bytes 49160 | tf_op jit(solution)/shard_map/ppermute | solution.py:21
  546.9 11.0 %copy-start.11 = (f32[512,256]{0,1:S(1)}, f32[512,256]{0,1}, u32[]{:S(2)}) copy-start(f32[512,256]{0,1} %fusion.113) | copy-start | bytes 1572868
  561.8 9.4 %copy-start.6 = (f32[34,32,128]{2,1,0:T(8,128)S(1)}, f32[34,32,128]{2,1,0:T(8,128)}, u32[]{:S(2)}) copy-start(f32[34,32,128]{2,1,0:T(8,128)} %copy-done.5) | copy-start | bytes 1671172
  566.6 21.7 %all-to-all-start.7 = ((f32[16,1,16384]{2,1,0:T(1,128)}), f32[16,1,16384]{2,1,0:T(1,128)}, u32[]{:S(2)}, u32[]{:S(2)}) async-start(f32[16,1,16384]{2,1,0:T(1,128)} %reshape.98), calls=%async_computation.7 | async-start | bytes 2097152 | tf_op jit(solution)/shard_map/all_to_all | solution.py:90
  571.2 14.2 %collective-permute-start.2 = (f32[34,1,128]{2,1,0:T(1,128)S(1)}, f32[34,1,128]{2,1,0:T(1,128)S(1)}, u32[]{:S(2)}, u32[]{:S(2)}) collective-permute-start(f32[34,1,128]{2,1,0:T(1,128)S(1)} %get-tuple-element.27), channel_id=1, source_target_pairs={{0,1},{1,2},{2,3},{3,4},{4,5},{5,6},{6,7},{7,8},{8,9},{9,10},{10,1... | collective-permute-start | bytes 52232 | tf_op jit(solution)/shard_map/ppermute | solution.py:18
  573.3 12.4 %collective-permute-start.3 = (f32[34,1,128]{2,1,0:T(1,128)S(1)}, f32[34,1,128]{2,1,0:T(1,128)S(1)}, u32[]{:S(2)}, u32[]{:S(2)}) collective-permute-start(f32[34,1,128]{2,1,0:T(1,128)S(1)} %get-tuple-element.26), channel_id=1, source_target_pairs={{1,0},{2,1},{3,2},{4,3},{5,4},{6,5},{7,6},{8,7},{9,8},{10,9},{11,1... | collective-permute-start | bytes 52232 | tf_op jit(solution)/shard_map/ppermute | solution.py:21
  595.9 11.2 %copy-start.7 = (f32[33,33,128]{2,1,0:T(8,128)S(1)}, f32[33,33,128]{2,1,0:T(8,128)}, u32[]{:S(2)}) copy-start(f32[33,33,128]{2,1,0:T(8,128)} %get-tuple-element.5) | copy-start | bytes 1672708
  601.9 11.3 %copy-start.1 = (f32[32,32,32]{2,1,0:T(8,128)S(1)}, f32[32,32,32]{2,1,0:T(8,128)}, u32[]{:S(2)}) copy-start(f32[32,32,32]{2,1,0:T(8,128)} %param.5) | copy-start | bytes 393220
  (5 other events, 22.8 us)
where the time goes:
time: 619 us; the launch traced here: 613 us
  matrix products  216 us (35%)
  local copies, waits for them, and re-layouts  159 us (26%)
  blocking collectives  106 us (17%)
  waiting for transfers between devices  62.9 us (10%)
  starting transfers between devices  38.6 us (6%)
  other arithmetic  29.9 us (5%)
    dot_general x42, matrix products, product(): return jnp.einsum(pattern, left, right, precision=lax.Precision.HIGHEST)  171 us
    unnamed x60, local copies, waits for them, and re-layouts  57.8 us
    unnamed x8, matrix products  44.8 us
    all_to_all x1, blocking collectives, outward_two(): lax.all_to_all(spectrum, 'px', split_axis=2, concat_axis=3, tiled=True)  34.2 us
    all_to_all x1, blocking collectives, homeward_two(): lax.all_to_all(spectrum, 'px', split_axis=3, concat_axis=2, tiled=True)  33.3 us
    all_to_all x1, waiting for transfers between devices, outward_two(): lax.all_to_all(spectrum, 'px', split_axis=2, concat_axis=3, tiled=True)  20.9 us
    all_to_all x1, blocking collectives, homeward_one(): lax.all_to_all(spectrum, 'py', split_axis=3, concat_axis=2, tiled=True)  19.6 us
    all_to_all x1, blocking collectives, outward_one(): lax.all_to_all(spectrum, 'py', split_axis=2, concat_axis=3, tiled=True)  19.2 us
  transfers between devices with their start and end apart: 8, of which 6 were waited for; matrix products, arithmetic and copies ran while one was open for 2% of the time, Pallas kernels for 0%

commit v1 on v0

--- a/solution.py
+++ b/solution.py
@@ -77,7 +77,10 @@
 
 
 def outward_two(spectrum):
-    result = lax.all_to_all(spectrum, "px", split_axis=2, concat_axis=3, tiled=True)
+    result = jnp.concatenate(
+        lax.all_to_all(jnp.stack(jnp.split(spectrum, lax.axis_size("px"), axis=2)), "px", 0, 0),
+        axis=3,
+    )
     return result
 
 

time: 619 us -> 625 us (level)
    all_to_all x2 -> x0, local copies, waits for them, and re-layouts: 9.23 us -> none  [outward_two(): lax.all_to_all(spectrum, 'px', split_axis=2, concat_axis=3, tiled=True)]
    another operation x2 -> x0, local copies, waits for them, and re-layouts: 7.32 us -> none  [along_first(): return jnp.stack([real_part, imag_part])]
    unnamed x60 -> x66, local copies, waits for them, and re-layouts: 57.8 us -> 62.5 us
where the time goes in v1:
time: 625 us; the launch traced here: 619 us
  matrix products  218 us (35%)
  local copies, waits for them, and re-layouts  160 us (26%)
  blocking collectives  106 us (17%)
  waiting for transfers between devices  62.9 us (10%)
  starting transfers between devices  38.5 us (6%)
  other arithmetic  32.7 us (5%)
    dot_general x42, matrix products, product(): return jnp.einsum(pattern, left, right, precision=lax.Precision.HIGHEST)  172 us
    unnamed x66, local copies, waits for them, and re-layouts  62.5 us
    unnamed x8, matrix products  45.3 us
    all_to_all x1, blocking collectives, outward_two(): lax.all_to_all(jnp.stack(jnp.split(spectrum, lax.axis_size('px'), axis=2)...  34.1 us
    all_to_all x1, blocking collectives, homeward_two(): lax.all_to_all(spectrum, 'px', split_axis=3, concat_axis=2, tiled=True)  33.3 us
    all_to_all x1, waiting for transfers between devices, outward_two(): lax.all_to_all(jnp.stack(jnp.split(spectrum, lax.axis_size('px'), axis=2)...  20.9 us
    all_to_all x1, blocking collectives, outward_one(): lax.all_to_all(spectrum, 'py', split_axis=2, concat_axis=3, tiled=True)  19.4 us
    all_to_all x1, blocking collectives, homeward_one(): lax.all_to_all(spectrum, 'py', split_axis=3, concat_axis=2, tiled=True)  19.4 us
  transfers between devices with their start and end apart: 8, of which 6 were waited for; matrix products, arithmetic and copies ran while one was open for 2% of the time, Pallas kernels for 0%

profile of v1, /device:TPU:2, one launch (start us, length us, event | category | flops | bytes accessed | tf_op | source)
XLA Modules:
  0.0 619.2 jit_solution(11606695566176006822)
XLA Ops:
  13.1 6.2 %all-to-all-start = ((f32[16,1,16384]{2,1,0:T(1,128)}), f32[16,1,16384]{2,1,0:T(1,128)S(1)}, u32[]{:S(2)}, u32[]{:S(2)}) async-start(f32[16,1,16384]{2,1,0:T(1,128)} %reshape.94), calls=%async_computation | async-start | bytes 2097152 | tf_op jit(solution)/shard_map/all_to_all | solution.py:75
  21.6 12.0 %all-to-all-done = f32[16,1,16384]{2,1,0:T(1,128)S(1)} async-done(((f32[16,1,16384]{2,1,0:T(1,128)}), f32[16,1,16384]{2,1,0:T(1,128)S(1)}, u32[]{:S(2)}, u32[]{:S(2)}) %all-to-all-start) | async-done | bytes 1048608 | tf_op jit(solution)/shard_map/all_to_all | solution.py:75
  47.6 6.4 %fusion.57 = f32[512,32,8]{0,1,2:T(8,128)} fusion(f32[32,8,512]{2,0,1:T(8,128)S(1)} %squeeze.49), kind=kOutput, calls=%fused_computation.159 | convolution fusion | flops 808976384 | bytes 1048576 | tf_op jit(solution)/shard_map/bza,ak->zkb/dot_general | solution.py:27
  56.0 6.5 %fusion.59 = f32[512,32,8]{0,1,2:T(8,128)S(1)} fusion(f32[32,8,512]{2,0,1:T(8,128)} %squeeze.48), kind=kOutput, calls=%fused_computation.161 | convolution fusion | flops 808976384 | bytes 1048576 | tf_op jit(solution)/shard_map/bza,ak->zkb/dot_general | solution.py:27
  81.7 11.1 %all-to-all-start.1 = ((f32[16,1,16384]{2,1,0:T(1,128)}), f32[16,1,16384]{2,1,0:T(1,128)S(1)}, u32[]{:S(2)}, u32[]{:S(2)}) async-start(f32[16,1,16384]{2,1,0:T(1,128)} %reshape.96), calls=%async_computation.1 | async-start | bytes 2097152 | tf_op jit(solution)/shard_map/all_to_all | solution.py:81
  101.8 20.9 %all-to-all-done.1 = f32[16,1,16384]{2,1,0:T(1,128)S(1)} async-done(((f32[16,1,16384]{2,1,0:T(1,128)}), f32[16,1,16384]{2,1,0:T(1,128)S(1)}, u32[]{:S(2)}, u32[]{:S(2)}) %all-to-all-start.1) | async-done | bytes 1048608 | tf_op jit(solution)/shard_map/all_to_all | solution.py:81
  136.9 6.0 fusion.55
  191.8 33.3 %all_to_all.100 = f32[16,1,16384]{2,1,0:T(1,128)S(1)} all-to-all(f32[16,1,16384]{2,1,0:T(1,128)S(1)} %reshape.98), channel_id=1, replica_groups=mesh['px'=16,'py'=16] {'px'}, dimensions={0} | all-to-all | bytes 2097152 | tf_op jit(solution)/shard_map/all_to_all | solution.py:88
  239.6 5.9 fusion.109
  245.5 5.7 fusion.91
  270.7 19.4 %all_to_all.101 = f32[16,1,16384]{2,1,0:T(1,128)S(1)} all-to-all(f32[16,1,16384]{2,1,0:T(1,128)S(1)} %reshape.100), channel_id=1, replica_groups=mesh['px'=16,'py'=16] {'py'}, dimensions={0} | all-to-all | bytes 2097152 | tf_op jit(solution)/shard_map/all_to_all | solution.py:93
  295.9 6.1 copy.69
  322.3 19.4 %all_to_all.102 = f32[16,1,16384]{2,1,0:T(1,128)S(1)} all-to-all(f32[16,1,16384]{2,1,0:T(1,128)S(1)} %reshape.102), channel_id=1, replica_groups=mesh['px'=16,'py'=16] {'py'}, dimensions={0} | all-to-all | bytes 2097152 | tf_op jit(solution)/shard_map/all_to_all | solution.py:75
  355.1 5.9 fusion.45
  368.6 6.4 %fusion.6 = f32[1,8,512,32]{2,3,1,0:T(8,128)S(1)} fusion(f32[512,32,8]{0,1,2:T(8,128)S(1)} %copy-done.22, f32[32,8,512]{2,0,1:T(8,128)} %copy-done.15), kind=kOutput, calls=%fused_computation.85 | convolution fusion | flops 809107456 | bytes 1572864 | tf_op jit(solution)/shard_map/bza,ak->zkb/dot_general | solution.py:27
  388.0 34.1 %all_to_all.103 = f32[16,1,16384]{2,1,0:T(1,128)S(1)} all-to-all(f32[16,1,16384]{2,1,0:T(1,128)S(1)} %reshape.104), channel_id=1, replica_groups=mesh['px'=16,'py'=16] {'px'}, dimensions={0} | all-to-all | bytes 2097152 | tf_op jit(solution)/shard_map/all_to_all | solution.py:81
  436.3 5.8 fusion.43
  508.7 16.5 %all-to-all-done.6 = f32[16,1,16384]{2,1,0:T(1,128)S(1)} async-done(((f32[16,1,16384]{2,1,0:T(1,128)}), f32[16,1,16384]{2,1,0:T(1,128)S(1)}, u32[]{:S(2)}, u32[]{:S(2)}) %all-to-all-start.6) | async-done | bytes 1048608 | tf_op jit(solution)/shard_map/all_to_all | solution.py:88
  539.9 5.9 fusion.113
  545.8 5.8 fusion.95
  552.4 5.8 fusion.93
  583.6 7.7 %collective-permute-done.2 = f32[34,1,128]{2,1,0:T(1,128)S(1)} collective-permute-done((f32[34,1,128]{2,1,0:T(1,128)S(1)}, f32[34,1,128]{2,1,0:T(1,128)S(1)}, u32[]{:S(2)}, u32[]{:S(2)}) %collective-permute-start.2) | collective-permute-done | bytes 17440 | tf_op jit(solution)/shard_map/ppermute | solution.py:18
  601.6 6.1 copy.81
  612.9 6.2 fusion.19
  (213 shorter events, 352.9 us)
Async XLA Ops:
  0.0 19.3 %copy-start = (f32[32,32,32]{2,1,0:T(8,128)S(1)}, f32[32,32,32]{2,1,0:T(8,128)}, u32[]{:S(2)}) copy-start(f32[32,32,32]{2,1,0:T(8,128)} %param.5) | copy-start | bytes 393220
  13.1 20.5 %all-to-all-start = ((f32[16,1,16384]{2,1,0:T(1,128)}), f32[16,1,16384]{2,1,0:T(1,128)S(1)}, u32[]{:S(2)}, u32[]{:S(2)}) async-start(f32[16,1,16384]{2,1,0:T(1,128)} %reshape.94), calls=%async_computation | async-start | bytes 2097152 | tf_op jit(solution)/shard_map/all_to_all | solution.py:75
  47.6 6.4 %copy-start.3 = (f32[1,32,8,16,32]{4,2,3,1,0:T(8,128)S(1)}, f32[1,32,8,16,32]{4,2,3,1,0:T(8,128)}, u32[]{:S(2)}) copy-start(f32[1,32,8,16,32]{4,2,3,1,0:T(8,128)} %get-tuple-element.19) | copy-start | bytes 1572868
  56.0 6.5 %copy-start.14 = (f32[32,8,512]{2,0,1:T(8,128)S(1)}, f32[32,8,512]{2,0,1:T(8,128)}, u32[]{:S(2)}) copy-start(f32[32,8,512]{2,0,1:T(8,128)} %squeeze.48) | copy-start | bytes 1572868
  56.0 6.5 %copy-start.20 = (f32[512,32,8]{0,1,2:T(8,128)S(1)}, f32[512,32,8]{0,1,2:T(8,128)}, u32[]{:S(2)}) copy-start(f32[512,32,8]{0,1,2:T(8,128)} %fusion.57) | copy-start | bytes 1572868
  81.7 40.9 %all-to-all-start.1 = ((f32[16,1,16384]{2,1,0:T(1,128)}), f32[16,1,16384]{2,1,0:T(1,128)S(1)}, u32[]{:S(2)}, u32[]{:S(2)}) async-start(f32[16,1,16384]{2,1,0:T(1,128)} %reshape.96), calls=%async_computation.1 | async-start | bytes 2097152 | tf_op jit(solution)/shard_map/all_to_all | solution.py:81
  146.0 10.7 %copy-start.16 = (f32[8,32,512]{2,1,0:T(8,128)S(1)}, f32[8,32,512]{2,1,0:T(8,128)}, u32[]{:S(2)}) copy-start(f32[8,32,512]{2,1,0:T(8,128)} %fusion.16) | copy-start | bytes 1572868
  146.0 10.7 %copy-start.18 = (f32[8,32,512]{2,1,0:T(8,128)S(1)}, f32[8,32,512]{2,1,0:T(8,128)}, u32[]{:S(2)}) copy-start(f32[8,32,512]{2,1,0:T(8,128)} %fusion.17) | copy-start | bytes 1572868
  252.0 10.8 %copy-start.12 = (f32[512,256]{0,1:S(1)}, f32[512,256]{0,1}, u32[]{:S(2)}) copy-start(f32[512,256]{0,1} %fusion.109) | copy-start | bytes 1572868
  295.9 11.2 %copy-start.10 = (f32[32,32,128]{2,1,0:T(8,128)S(1)}, f32[32,32,128]{2,1,0:T(8,128)}, u32[]{:S(2)}) copy-start(f32[32,32,128]{2,1,0:T(8,128)} %param.4) | copy-start | bytes 1572868
  355.1 5.9 copy-start.4
  445.2 11.1 %copy-start.17 = (f32[8,32,512]{2,1,0:T(8,128)S(1)}, f32[8,32,512]{2,1,0:T(8,128)}, u32[]{:S(2)}) copy-start(f32[8,32,512]{2,1,0:T(8,128)} %fusion.16) | copy-start | bytes 1572868
  445.2 11.1 %copy-start.19 = (f32[8,32,512]{2,1,0:T(8,128)S(1)}, f32[8,32,512]{2,1,0:T(8,128)}, u32[]{:S(2)}) copy-start(f32[8,32,512]{2,1,0:T(8,128)} %fusion.17) | copy-start | bytes 1572868
  487.1 8.5 %copy-start.2 = (f32[32,32,128]{2,1,0:T(8,128)S(1)}, f32[32,32,128]{2,1,0:T(8,128)}, u32[]{:S(2)}) copy-start(f32[32,32,128]{2,1,0:T(8,128)} %param.3) | copy-start | bytes 1572868
  491.9 33.3 %all-to-all-start.6 = ((f32[16,1,16384]{2,1,0:T(1,128)}), f32[16,1,16384]{2,1,0:T(1,128)S(1)}, u32[]{:S(2)}, u32[]{:S(2)}) async-start(f32[16,1,16384]{2,1,0:T(1,128)} %reshape.106), calls=%async_computation.6 | async-start | bytes 2097152 | tf_op jit(solution)/shard_map/all_to_all | solution.py:88
  495.6 6.6 %collective-permute-start = (f32[1,32,128]{2,1,0:T(8,128)S(1)}, f32[1,32,128]{2,1,0:T(8,128)S(1)}, u32[]{:S(2)}, u32[]{:S(2)}) collective-permute-start(f32[1,32,128]{2,1,0:T(8,128)S(1)} %get-tuple-element.29), channel_id=1, source_target_pairs={{0,16},{16,32},{32,48},{48,64},{64,80},{80,96},{96,112},{112,128},... | collective-permute-start | bytes 49160 | tf_op jit(solution)/shard_map/ppermute | solution.py:18
  500.8 7.1 %collective-permute-start.1 = (f32[1,32,128]{2,1,0:T(8,128)S(1)}, f32[1,32,128]{2,1,0:T(8,128)S(1)}, u32[]{:S(2)}, u32[]{:S(2)}) collective-permute-start(f32[1,32,128]{2,1,0:T(8,128)S(1)} %get-tuple-element.28), channel_id=1, source_target_pairs={{16,0},{32,16},{48,32},{64,48},{80,64},{96,80},{112,96},{128,112},... | collective-permute-start | bytes 49160 | tf_op jit(solution)/shard_map/ppermute | solution.py:21
  552.4 11.2 %copy-start.13 = (f32[512,256]{0,1:S(1)}, f32[512,256]{0,1}, u32[]{:S(2)}) copy-start(f32[512,256]{0,1} %fusion.113) | copy-start | bytes 1572868
  567.6 9.4 %copy-start.8 = (f32[34,32,128]{2,1,0:T(8,128)S(1)}, f32[34,32,128]{2,1,0:T(8,128)}, u32[]{:S(2)}) copy-start(f32[34,32,128]{2,1,0:T(8,128)} %copy-done.7) | copy-start | bytes 1671172
  572.4 21.7 %all-to-all-start.7 = ((f32[16,1,16384]{2,1,0:T(1,128)}), f32[16,1,16384]{2,1,0:T(1,128)}, u32[]{:S(2)}, u32[]{:S(2)}) async-start(f32[16,1,16384]{2,1,0:T(1,128)} %reshape.108), calls=%async_computation.7 | async-start | bytes 2097152 | tf_op jit(solution)/shard_map/all_to_all | solution.py:93
  577.1 14.2 %collective-permute-start.2 = (f32[34,1,128]{2,1,0:T(1,128)S(1)}, f32[34,1,128]{2,1,0:T(1,128)S(1)}, u32[]{:S(2)}, u32[]{:S(2)}) collective-permute-start(f32[34,1,128]{2,1,0:T(1,128)S(1)} %get-tuple-element.27), channel_id=1, source_target_pairs={{0,1},{1,2},{2,3},{3,4},{4,5},{5,6},{6,7},{7,8},{8,9},{9,10},{10,1... | collective-permute-start | bytes 52232 | tf_op jit(solution)/shard_map/ppermute | solution.py:18
  579.1 12.4 %collective-permute-start.3 = (f32[34,1,128]{2,1,0:T(1,128)S(1)}, f32[34,1,128]{2,1,0:T(1,128)S(1)}, u32[]{:S(2)}, u32[]{:S(2)}) collective-permute-start(f32[34,1,128]{2,1,0:T(1,128)S(1)} %get-tuple-element.26), channel_id=1, source_target_pairs={{1,0},{2,1},{3,2},{4,3},{5,4},{6,5},{7,6},{8,7},{9,8},{10,9},{11,1... | collective-permute-start | bytes 52232 | tf_op jit(solution)/shard_map/ppermute | solution.py:21
  601.6 11.2 %copy-start.9 = (f32[33,33,128]{2,1,0:T(8,128)S(1)}, f32[33,33,128]{2,1,0:T(8,128)}, u32[]{:S(2)}) copy-start(f32[33,33,128]{2,1,0:T(8,128)} %get-tuple-element.5) | copy-start | bytes 1672708
  607.7 11.3 %copy-start.1 = (f32[32,32,32]{2,1,0:T(8,128)S(1)}, f32[32,32,32]{2,1,0:T(8,128)}, u32[]{:S(2)}) copy-start(f32[32,32,32]{2,1,0:T(8,128)} %param.5) | copy-start | bytes 393220
  (8 other events, 27.7 us)
